TPU v7x, 256 devices: a whole 4x4x8 slice. The times are simulated.
256 devices in a mesh: pair: 64 (over y, z, x_hi), day: 4 (over x_lo, core).
Axes of the slice: x: 4 (x_hi: 2, x_lo: 2; x = x_hi * 2 + x_lo), y: 4, z: 8, core: 2. Of those that a mesh axis runs over, the one named last changes fastest.
Arguments:
- spectra: bfloat16 [8, 64, 128, 8192], P('day', 'pair'), may hold values from -6 to 6
- pair_mask: int32 [64, 2], P('pair'), may hold values 0 or 1
- window_of_day: int32 [8], replicated, may hold values from 0 to 1, as said below
- band_weight: float32 [8], replicated, may hold values from 0.5 to 4
Outputs:
- gradient: bfloat16 [8, 64, 128, 8192], P('day', 'pair')
Inputs may be any that keep to these rules, and one draw needn't show every extreme that they name: `window_of_day`: window 0 holds exactly 2 days, window 1 the other 6.
All inputs are finite; a program needn't handle non-finite values. No bound on the sum of `pair_mask` on one device may be relied on, other than what follows from the above.
Results may differ from a plain program's by a relative error of at most 0.012.
Values may be sent and summed in bfloat16 or wider, within the bound.
No kernel may reach another device: no remote copies, remote signals or barrier semaphores. Data moves between devices by JAX's collectives and lax.ppermute only.
A program may use at most 128 MiB of HBM per device.

v0:
```python
import jax
import jax.numpy as jnp
from jax import lax
from jax.sharding import PartitionSpec as P

NBAND = 8


def from_behind(x, axis, by):
    peers = lax.axis_size(axis)
    pairs = [(i, i + by) for i in range(peers) if 0 <= i + by < peers]
    return lax.ppermute(x, axis, pairs)


def shards(spectra, pair_mask, window_of_day, band_weight):
    day_dev, single_block, stations, row_width = spectra.shape
    band_bins = row_width // (2 * NBAND)
    norm_scale = (2.0 * band_bins) ** (-0.5)
    reach_count = pair_mask.shape[1]
    field_shape = (day_dev, stations, 2, NBAND, band_bins)
    home_blocks = spectra.reshape(field_shape)
    count_first = jnp.sum((window_of_day == 0).astype(jnp.float32))
    count_second = jnp.sum((window_of_day == 1).astype(jnp.float32))
    first_day = lax.axis_index("day") * day_dev
    local_windows = lax.dynamic_slice_in_dim(window_of_day, first_day, day_dev)
    day_weight = jnp.where(local_windows == 0, 1.0 / count_first, -1.0 / count_second)
    partner_list = []
    power_list = []
    for offset in range(1, reach_count + 1):
        partner = from_behind(spectra, "pair", -offset).reshape(field_shape)
        partner_list.append(partner)
        band_power = jnp.einsum(
            "dicnf,djcnf->dnij", home_blocks, partner, preferred_element_type=jnp.float32
        )
        power_list.append(jnp.einsum("d,dnij->nij", day_weight, band_power * norm_scale))
    stacked = jnp.stack(power_list, axis=0)
    difference = lax.psum(stacked, "day")
    difference = difference * pair_mask[0].astype(jnp.float32)[:, None, None, None]
    weighted = (band_weight[None, :, None, None] * difference).astype(jnp.bfloat16)
    gradient = jnp.zeros(field_shape, jnp.float32)
    for offset in range(1, reach_count + 1):
        gradient = gradient + jnp.einsum(
            "nij,djcnf->dicnf",
            weighted[offset - 1],
            partner_list[offset - 1],
            preferred_element_type=jnp.float32,
        )
    for offset in range(1, reach_count + 1):
        partner_term = jnp.einsum(
            "nij,dicnf->djcnf",
            weighted[offset - 1],
            home_blocks,
            preferred_element_type=jnp.float32,
        )
        gradient = gradient + from_behind(partner_term, "pair", offset)
    gradient = gradient * (day_weight * norm_scale)[:, None, None, None, None]
    return gradient.astype(jnp.bfloat16).reshape(spectra.shape)


def solution(mesh):
    return jax.shard_map(
        shards,
        mesh=mesh,
        in_specs=(P("day", "pair", None, None), P("pair", None), P(), P()),
        out_specs=P("day", "pair", None, None),
        check_vma=False,
    )
```

profile of v0, /device:TPU:14, one launch (start us, length us, event | category | flops | bytes accessed | tf_op | source)
XLA Modules:
  0.0 908.6 jit_solution(12109033763661348392)
XLA Ops:
  6.5 6.3 copy.9
  12.9 3.3 collective-permute-start
  16.2 7.7 collective-permute-start.1
  23.8 6.1 copy.42
  29.9 0.6 fusion.49
  31.9 79.0 %collective-permute-done = bf16[2,1,128,8192]{2,3,0,1:T(8,128)(2,1)} collective-permute-done((bf16[2,1,128,8192]{2,3,0,1:T(8,128)(2,1)}, bf16[2,1,128,8192]{2,3,0,1:T(8,128)(2,1)}, u32[]{:S(2)}, u32[]{:S(2)}) %collective-permute-start) | collective-permute-done | bytes 4194336 | tf_op jit(solution)/shard_map/ppermute | solution.py:12
  110.9 8.5 fusion.40
  119.4 83.5 %collective-permute-done.1 = bf16[2,1,128,8192]{2,3,0,1:T(8,128)(2,1)} collective-permute-done((bf16[2,1,128,8192]{2,3,0,1:T(8,128)(2,1)}, bf16[2,1,128,8192]{2,3,0,1:T(8,128)(2,1)}, u32[]{:S(2)}, u32[]{:S(2)}) %collective-permute-start.1) | collective-permute-done | bytes 4194336 | tf_op jit(solution)/shard_map/ppermute | solution.py:12
  202.9 7.3 fusion.35
  210.2 0.7 fusion.47
  210.9 0.7 fusion.45
  211.6 1.1 pad_maximum_fusion
  212.8 121.9 %all-reduce.2.cloned.1.call-done = f32[2,8,128,128]{3,2,1,0:T(8,128)} async-done(((f32[2,8,128,128]{3,2,1,0:T(8,128)}), f32[2,8,128,128]{3,2,1,0:T(8,128)}) %all-reduce.2.cloned.1.call-update) | async-done | bytes 1048592 | tf_op jit(solution)/shard_map/psum | solution.py:37
  334.7 1.4 multiply_convert_fusion
  336.1 7.7 fusion.17
  343.9 5.4 fusion.20
  349.3 4.5 collective-permute-start.2
  353.7 3.7 collective-permute-start.3
  357.4 6.7 fusion.3
  364.1 171.2 %collective-permute-done.2 = f32[2,128,2,8,512]{4,1,2,0,3:T(8,128)} collective-permute-done((f32[2,128,2,8,512]{4,1,2,0,3:T(8,128)S(1)}, f32[2,128,2,8,512]{4,1,2,0,3:T(8,128)}, u32[]{:S(2)}, u32[]{:S(2)}) %collective-permute-start.2) | collective-permute-done | bytes 8388640 | tf_op jit(solution)/shard_map/ppermute | solution.py:12
  535.3 340.8 %collective-permute-done.3 = f32[2,128,2,8,512]{4,1,2,0,3:T(8,128)} collective-permute-done((f32[2,128,2,8,512]{4,1,2,0,3:T(8,128)S(1)}, f32[2,128,2,8,512]{4,1,2,0,3:T(8,128)}, u32[]{:S(2)}, u32[]{:S(2)}) %collective-permute-start.3) | collective-permute-done | bytes 8388640 | tf_op jit(solution)/shard_map/ppermute | solution.py:12
  876.1 13.1 %fusion.2 = bf16[2,128,2,8,512]{4,1,2,0,3:T(8,128)(2,1)} fusion(f32[2,128,2,8,512]{4,1,2,0,3:T(8,128)} %collective-permute-done.3, f32[2,128,2,8,512]{4,1,2,0,3:T(8,128)} %collective-permute-done.2, f32[8,128,2,2,512]{4,1,3,2,0:T(8,128)} %fusion.3, f32[2]{0:T(128)S(1)} %get-tuple-element.7, bf16[2,128,2,8,512]{1,4,3,2,0:T(8,128)(2,1)} %bitcast.2, ...), kind=kOutput, calls=%fused_computation.3 | convolution fusion | flops 547356672 | bytes 33817088 | tf_op jit(solution)/shard_map/nij,djcnf->dicnf/dot_general | solution.py:42
  889.2 6.2 copy.17
  895.4 6.3 copy.18
  (14 shorter events, 0.1 us)
Async XLA Ops:
  6.5 328.2 %all-reduce.2.cloned.1.call-start = ((), (), s32[]{:S(2)}) async-start(), calls=%async_computation | async-start | bytes 2097152 | tf_op jit(solution)/shard_map/psum | solution.py:37
  12.9 98.0 %collective-permute-start = (bf16[2,1,128,8192]{2,3,0,1:T(8,128)(2,1)}, bf16[2,1,128,8192]{2,3,0,1:T(8,128)(2,1)}, u32[]{:S(2)}, u32[]{:S(2)}) collective-permute-start(bf16[2,1,128,8192]{2,3,0,1:T(8,128)(2,1)} %copy.9), channel_id=1, source_target_pairs={{4,0},{8,4},{12,8},{16,12},{20,16},{24,20},{28,24},{32,28},{36,32}... | collective-permute-start | bytes 12582920 | tf_op jit(solution)/shard_map/ppermute | solution.py:12
  16.2 186.7 %collective-permute-start.1 = (bf16[2,1,128,8192]{2,3,0,1:T(8,128)(2,1)}, bf16[2,1,128,8192]{2,3,0,1:T(8,128)(2,1)}, u32[]{:S(2)}, u32[]{:S(2)}) collective-permute-start(bf16[2,1,128,8192]{2,3,0,1:T(8,128)(2,1)} %copy.9), channel_id=1, source_target_pairs={{8,0},{12,4},{16,8},{20,12},{24,16},{28,20},{32,24},{36,28},{40,32... | collective-permute-start | bytes 12582920 | tf_op jit(solution)/shard_map/ppermute | solution.py:12
  23.8 6.1 copy-start.3
  110.9 92.0 %copy-start = (bf16[32,8,16,512]{3,2,1,0:T(8,128)(2,1)S(1)}, bf16[32,8,16,512]{3,2,1,0:T(8,128)(2,1)}, u32[]{:S(2)}) copy-start(bf16[32,8,16,512]{3,2,1,0:T(8,128)(2,1)} %copy.42) | copy-start | bytes 12582916
  210.2 2.5 copy-start.4
  210.2 124.5 %copy-start.2 = (f32[8]{0:T(128)S(1)}, f32[8]{0:T(128)}, u32[]{:S(2)}) copy-start(f32[8]{0:T(128)} %param.7) | copy-start | bytes 100
  336.1 7.7 copy-start.1
  349.3 186.1 %collective-permute-start.2 = (f32[2,128,2,8,512]{4,1,2,0,3:T(8,128)S(1)}, f32[2,128,2,8,512]{4,1,2,0,3:T(8,128)}, u32[]{:S(2)}, u32[]{:S(2)}) collective-permute-start(f32[2,128,2,8,512]{4,1,2,0,3:T(8,128)S(1)} %fusion.17), channel_id=1, source_target_pairs={{0,4},{4,8},{8,12},{12,16},{16,20},{20,24},{24,28},{28,32},{32,36}... | collective-permute-start | bytes 25165832 | tf_op jit(solution)/shard_map/ppermute | solution.py:12
  353.7 522.4 %collective-permute-start.3 = (f32[2,128,2,8,512]{4,1,2,0,3:T(8,128)S(1)}, f32[2,128,2,8,512]{4,1,2,0,3:T(8,128)}, u32[]{:S(2)}, u32[]{:S(2)}) collective-permute-start(f32[2,128,2,8,512]{4,1,2,0,3:T(8,128)S(1)} %fusion.20), channel_id=1, source_target_pairs={{0,8},{4,12},{8,16},{12,20},{16,24},{20,28},{24,32},{28,36},{32,40... | collective-permute-start | bytes 25165832 | tf_op jit(solution)/shard_map/ppermute | solution.py:12
Sparse Core Ops, SparseCore 0:
  212.8 121.8 all-reduce.1
where the time goes:
time: 909 us
  waiting for transfers between devices  796 us (88%)
  matrix products  50 us (6%)
  local copies, waits for them, and re-layouts  24.9 us (3%)
  starting transfers between devices  19.1 us (2%)
  between operations  14.8 us (2%)
    ppermute x4, waiting for transfers between devices, from_behind(): return lax.ppermute(x, axis, pairs)  674 us
    psum x1, waiting for transfers between devices, shards(): difference = lax.psum(stacked, 'day')  122 us
    dot_general x2, matrix products, shards(): jnp.einsum('nij,djcnf->dicnf', weighted[offset - 1], partner_list[offset...  19.8 us
    ppermute x4, starting transfers between devices, from_behind(): return lax.ppermute(x, axis, pairs)  19.1 us
  transfers between devices with their start and end apart: 5, of which 5 were waited for; matrix products, arithmetic and copies ran while one was open for 2% of the time, Pallas kernels for 0%

commit v1 on v0

v1 whole, which is shorter than its diff:
```python
import jax
import jax.numpy as jnp
from jax import lax
from jax.experimental import pallas as pl
from jax.experimental.pallas import tpu as pltpu
from jax.sharding import Mesh
from jax.sharding import PartitionSpec as P

NBAND = 8
RING = 4
TAGS = 2
MASK_ROWS = 8
SENT = (1, 3, 2)
RING_AXES = ("xh", "xl")
ANY = pl.BlockSpec(memory_space=pl.ANY)
SMEM = pl.BlockSpec(memory_space=pltpu.SMEM)


def call(kernel, vmem=16 << 20, **how):
    return pl.pallas_call(kernel, compiler_params=pltpu.CompilerParams(vmem_limit_bytes=vmem), **how)


def ring_place():
    return lax.axis_index("xh") * 2 + lax.axis_index("xl")


def column_start(tag, k, c, bins):
    band = RING * tag + (ring_place() ^ k)
    return pl.multiple_of(c * NBAND * bins + band * bins, bins)


def pack(spectra, pair_mask, wanted):
    days, _, stations, width = spectra.shape
    bins = width // (2 * NBAND)
    rows = days * stations
    count = sum(len(pieces) for pieces, _ in wanted)
    masked = any(mask for _, mask in wanted)

    def kernel(x_ref, m_ref, *refs):
        outs = refs[: len(wanted)]
        held, slab, in_sem, out_sem, slab_sem = refs[len(wanted) :]
        loads, stores, at = [], [], 0
        for pieces, _ in wanted:
            for tag, k in pieces:
                for c in range(2):
                    for d in range(days):
                        load = pltpu.make_async_copy(
                            x_ref.at[d, 0, :, pl.ds(column_start(tag, k, c, bins), bins)],
                            held.at[at, pl.ds(d * stations, stations), pl.ds(c * bins, bins)],
                            in_sem.at[at, c, d],
                        )
                        load.start()
                        loads.append(load)
                at += 1
        if masked:
            row = lax.broadcasted_iota(jnp.int32, slab.shape, 0)
            first, second = m_ref[0, 0].astype(jnp.float32), m_ref[0, 1].astype(jnp.float32)
            value = jnp.where(row == 0, first, jnp.where(row == 1, second, 0.0))
            slab[...] = value.astype(slab.dtype)
        at = 0
        for out, (pieces, mask) in zip(outs, wanted):
            for i in range(len(pieces)):
                for load in loads[2 * days * at : 2 * days * (at + 1)]:
                    load.wait()
                store = pltpu.make_async_copy(held.at[at], out.at[pl.ds(i * rows, rows), :], out_sem.at[at])
                store.start()
                stores.append(store)
                at += 1
        for j, (out, (pieces, mask)) in enumerate(zip(outs, wanted)):
            if mask:
                store = pltpu.make_async_copy(
                    slab, out.at[pl.ds(len(pieces) * rows, MASK_ROWS), :], slab_sem.at[j]
                )
                store.start()
                stores.append(store)
        for store in stores:
            store.wait()

    return call(
        kernel,
        out_shape=[
            jax.ShapeDtypeStruct((len(pieces) * rows + MASK_ROWS * mask, 2 * bins), spectra.dtype)
            for pieces, mask in wanted
        ],
        in_specs=[ANY, SMEM],
        out_specs=[ANY] * len(wanted),
        scratch_shapes=[
            pltpu.VMEM((count, rows, 2 * bins), spectra.dtype),
            pltpu.VMEM((MASK_ROWS, 2 * bins), spectra.dtype),
            pltpu.SemaphoreType.DMA((count, 2, days)),
            pltpu.SemaphoreType.DMA((count,)),
            pltpu.SemaphoreType.DMA((len(wanted),)),
        ],
        cost_estimate=pl.CostEstimate(flops=0, transcendentals=0, bytes_accessed=count << 20),
        vmem=60 << 20,
    )(spectra, pair_mask)


def join(pieces):
    rows = [p.shape[0] for p in pieces]
    starts = [sum(rows[:i]) for i in range(len(rows))]
    width, dtype = pieces[0].shape[1], pieces[0].dtype

    def kernel(*refs):
        ins, out, held, in_sem, out_sem = refs[:-4], *refs[-4:]
        spans = [pl.ds(start, n) for start, n in zip(starts, rows)]
        loads = [pltpu.make_async_copy(r, held.at[at, :], in_sem.at[i]) for i, (r, at) in enumerate(zip(ins, spans))]
        stores = [pltpu.make_async_copy(held.at[at, :], out.at[at, :], out_sem.at[i]) for i, at in enumerate(spans)]
        for load in loads:
            load.start()
        for load, store in zip(loads, stores):
            load.wait()
            store.start()
        for store in stores:
            store.wait()

    return call(
        kernel,
        out_shape=jax.ShapeDtypeStruct((sum(rows), width), dtype),
        in_specs=[ANY] * len(rows),
        out_specs=ANY,
        scratch_shapes=[
            pltpu.VMEM((sum(rows), width), dtype),
            pltpu.SemaphoreType.DMA((len(rows),)),
            pltpu.SemaphoreType.DMA((len(rows),)),
        ],
        cost_estimate=pl.CostEstimate(flops=0, transcendentals=0, bytes_accessed=3 << 20),
    )(*pieces)


def unpack(pieces, tag, shape, into=None):
    days, _, stations, width = shape
    bins = width // (2 * NBAND)
    dtype = pieces[0].dtype
    given = list(pieces) + ([] if into is None else [into])

    def kernel(*refs):
        ins, out_ref = refs[:RING], refs[len(given)]
        held, in_sem, out_sem = refs[len(given) + 1 :]
        loads, stores = [], []
        for k in range(RING):
            load = pltpu.make_async_copy(ins[k], held.at[k], in_sem.at[k])
            load.start()
            loads.append(load)
        for k in range(RING):
            loads[k].wait()
            for c in range(2):
                for d in range(days):
                    store = pltpu.make_async_copy(
                        held.at[k, pl.ds(d * stations, stations), pl.ds(c * bins, bins)],
                        out_ref.at[d, 0, :, pl.ds(column_start(tag, k, c, bins), bins)],
                        out_sem.at[k, c, d],
                    )
                    store.start()
                    stores.append(store)
        for store in stores:
            store.wait()

    return call(
        kernel,
        out_shape=jax.ShapeDtypeStruct(shape, dtype),
        in_specs=[ANY] * len(given),
        out_specs=ANY,
        scratch_shapes=[
            pltpu.VMEM((RING,) + pieces[0].shape, dtype),
            pltpu.SemaphoreType.DMA((RING,)),
            pltpu.SemaphoreType.DMA((RING, 2, days)),
        ],
        input_output_aliases={} if into is None else {RING: 0},
        cost_estimate=pl.CostEstimate(flops=0, transcendentals=0, bytes_accessed=4 << 20),
    )(*given)


def dot_nt(a, b):
    return lax.dot_general(a, b, (((1,), (1,)), ((), ())), preferred_element_type=jnp.float32)


def dot_nn(a, b):
    return lax.dot_general(a, b, (((1,), (0,)), ((), ())), preferred_element_type=jnp.float32)


def slot_blocks(sources, k, rows, cols):
    array, place = sources[k]
    return array, pl.BlockSpec((rows, cols), lambda j: (place, j))


def mask_blocks(array, width):
    place = array.shape[0] // MASK_ROWS - 1
    return array, pl.BlockSpec((MASK_ROWS, width), lambda j: (place, 0))


def stacked(tiles, n, day, stations):
    rows = pl.ds(day * stations, stations)
    return jnp.concatenate([tiles[n][rows, :], tiles[n + 1][rows, :]], axis=0)


def powers(day_weight, q, days, stations, sources, before=None):
    width = sources[0][0][0].shape[1]
    steps = 2
    cols = width // steps
    wide = 2 * stations
    extra = [] if before is None else [before]

    def kernel(w_ref, *refs):
        tiles, out = refs[:6], refs[-1]

        @pl.when(pl.program_id(0) == 0)
        def _():
            out[...] = jnp.zeros_like(out) if before is None else refs[6][...]

        up = down = side = 0.0
        for day in range(days):
            w = w_ref[q, day]
            mine, above, below = (stacked(tiles, n, day, stations) for n in (0, 2, 4))
            up += w * dot_nt(mine, above)
            down += w * dot_nt(mine, below)
            side += w * dot_nt(mine[:stations], mine)
        out[pl.ds(0, wide), :] += up
        out[pl.ds(wide, wide), :] += down
        out[pl.ds(2 * wide, stations), :] += side

    blocks = [slot_blocks(source, k, days * stations, cols) for source in sources for k in (q, q + 2)]
    shape = (5 * stations, wide)
    whole = pl.BlockSpec(shape, lambda j: (0, 0))
    return call(
        kernel,
        grid=(steps,),
        out_shape=jax.ShapeDtypeStruct(shape, jnp.float32),
        in_specs=[SMEM] + [spec for _, spec in blocks] + [whole] * len(extra),
        out_specs=whole,
        cost_estimate=pl.CostEstimate(
            flops=2 * wide * wide * 3 * width * days, transcendentals=0, bytes_accessed=4 << 20
        ),
    )(day_weight, *[a for a, _ in blocks], *extra)


def weigh(scale, mine, other, masks, stations):
    wide = 2 * stations

    def kernel(c_ref, p_ref, r_ref, here_a, here_b, below_a, below_b, out):
        top, bottom = pl.ds(0, stations), pl.ds(stations, stations)
        scale = c_ref[0]
        first = (lax.axis_index("xh") == 0).astype(jnp.float32)
        ha, hb, ba, bb = (
            m[...].astype(jnp.float32)[:, :stations] * scale for m in (here_a, here_b, below_a, below_b)
        )
        low = first * ha[0:1] + (1.0 - first) * hb[0:1]
        total = low * (p_ref[pl.ds(2 * wide, stations), bottom] + r_ref[pl.ds(2 * wide, stations), bottom])
        blank = jnp.zeros((stations, stations), out.dtype)
        out[0, top, top] = blank
        out[0, bottom, bottom] = blank
        out[0, top, bottom] = total.astype(out.dtype)
        out[0, bottom, top] = total.T.astype(out.dtype)
        column = lax.axis_index("h")
        has_next = (column < lax.axis_size("h") - 1).astype(jnp.float32)
        has_previous = (column > 0).astype(jnp.float32)
        ha, hb, ba, bb = has_next * ha, has_next * hb, has_previous * ba, has_previous * bb
        up = ((ha[1:2], (1.0 - first) * ha[0:1]), (first * hb[0:1], hb[1:2]))
        down = ((ba[1:2], first * bb[0:1]), ((1.0 - first) * ba[0:1], bb[1:2]))
        for way, factors in ((1, up), (2, down)):
            for i, rows in enumerate((top, bottom)):
                for j, columns in enumerate((top, bottom)):
                    at = pl.ds((way - 1) * wide + i * stations, stations)
                    total = factors[i][j] * (p_ref[at, columns] + r_ref[at, columns])
                    out[way, rows, columns] = total.astype(out.dtype)

    whole = pl.BlockSpec(mine.shape, lambda j: (0, 0))
    blocks = [mask_blocks(m, wide) for m in masks]
    return call(
        kernel,
        grid=(1,),
        out_shape=jax.ShapeDtypeStruct((3, wide, wide), jnp.bfloat16),
        in_specs=[SMEM, whole, whole] + [spec for _, spec in blocks],
        out_specs=pl.BlockSpec((3, wide, wide), lambda j: (0, 0, 0)),
        cost_estimate=pl.CostEstimate(flops=0, transcendentals=0, bytes_accessed=2 << 20),
    )(scale, mine, other, *[a for a, _ in blocks])


def gradients(day_scale, weighted, q, days, stations, sources):
    own = sources[0][0][0]
    width = own.shape[1]
    rows = days * stations
    steps = 2
    cols = width // steps
    wide = 2 * stations

    def kernel(w_ref, m_ref, *refs):
        tiles, outs = refs[:6], refs[6:]
        for day in range(days):
            mine, above, below = (stacked(tiles, n, day, stations) for n in (0, 2, 4))
            total = dot_nn(m_ref[0], mine) + dot_nn(m_ref[1], above) + dot_nn(m_ref[2], below)
            total = (w_ref[q, day] * total).astype(outs[0].dtype)
            outs[0][pl.ds(day * stations, stations), :] = total[:stations]
            outs[1][pl.ds(day * stations, stations), :] = total[stations:]

    blocks = [slot_blocks(source, k, rows, cols) for source in sources for k in (q, q + 2)]
    piece = pl.BlockSpec((rows, cols), lambda j: (0, j))
    return call(
        kernel,
        grid=(steps,),
        out_shape=[jax.ShapeDtypeStruct((rows, width), own.dtype)] * 2,
        in_specs=[SMEM, pl.BlockSpec(weighted.shape, lambda j: (0, 0, 0))] + [spec for _, spec in blocks],
        out_specs=[piece] * 2,
        cost_estimate=pl.CostEstimate(
            flops=2 * wide * wide * 3 * width * days, transcendentals=0, bytes_accessed=5 << 20
        ),
    )(day_scale, weighted, *[a for a, _ in blocks])


def ring_swap(x, k):
    return lax.ppermute(x, RING_AXES, [(i, i ^ k) for i in range(RING)])


def move_up(x, columns):
    return lax.ppermute(x, "h", [(i, (i + 1) % columns) for i in range(columns)])


def move_down(x, columns):
    return lax.ppermute(x, "h", [((i + 1) % columns, i) for i in range(columns)])


def core_swap(x):
    return lax.ppermute(x, "c", [(0, 1), (1, 0)])


def shards(spectra, pair_mask, window_of_day, band_weight):
    days, _, stations, width = spectra.shape
    columns = lax.axis_size("h")
    norm_scale = (2.0 * (width // (2 * NBAND))) ** (-0.5)
    count_first = jnp.sum((window_of_day == 0).astype(jnp.float32))
    count_second = jnp.sum((window_of_day == 1).astype(jnp.float32))
    all_weights = jnp.where(window_of_day == 0, 1.0 / count_first, -1.0 / count_second)
    by_device = all_weights.reshape(2, 2, days)
    on_core = lax.dynamic_index_in_dim(by_device, lax.axis_index("c"), 1, keepdims=False)
    day_weight = jnp.where(lax.axis_index("xl") == 0, on_core, on_core[::-1])
    day_scale = day_weight * norm_scale
    weights = band_weight.reshape(TAGS, RING) * norm_scale

    (own,) = pack(spectra, pair_mask, [(((0, 0), (1, 0)), True)])
    first = pack(spectra, pair_mask, [(((0, k),), k == 2) for k in SENT])
    second = pack(spectra, pair_mask, [(((1, k),), False) for k in SENT])
    here_own = [own, move_down(own, columns), move_up(own, columns)]
    sources, singles = [], []
    for tag, sent in enumerate((first, second)):
        came = [ring_swap(piece, k) for k, piece in zip(SENT, sent)]
        pair, single = join(came[:2]), came[2]
        pairs = [pair, move_down(pair, columns), move_up(pair, columns)]
        single = [single, move_down(single, columns), move_up(single, columns)]
        sources.append([((o, tag), (p, 0), (s, 0), (p, 1)) for o, p, s in zip(here_own, pairs, single)])
        singles.append(single)
    masks = [own, singles[0][0], here_own[2], singles[0][2]]
    out = None
    for tag in range(TAGS):
        mine = powers(day_weight, 1, days, stations, sources[tag])
        mine = powers(day_weight, 0, days, stations, sources[tag], mine)
        other = core_swap(mine)
        scale = lax.dynamic_index_in_dim(weights[tag], ring_place(), 0)
        weighted = weigh(scale, mine, other, masks, stations)
        grads = [None] * RING
        for q in (1, 0):
            grads[q], grads[q + 2] = gradients(day_scale, weighted, q, days, stations, sources[tag])
        moved = [grads[0]] + [ring_swap(grads[k], k) for k in range(1, RING)]
        out = unpack(moved, tag, spectra.shape, out)
    return out


def solution(mesh):
    columns = mesh.shape["pair"] // 2
    fine = Mesh(mesh.devices.reshape(columns, 2, 2, 2), ("h", "xh", "xl", "c"))
    return jax.shard_map(
        shards,
        mesh=fine,
        in_specs=(P(("xl", "c"), ("h", "xh"), None, None), P(("h", "xh"), None), P(), P()),
        out_specs=P(("xl", "c"), ("h", "xh"), None, None),
        check_vma=False,
    )
```

time: 909 us -> 201 us (0.22)
  waiting for transfers between devices: 796 us -> 106 us
  matrix products: 50 us -> 0 us
  Pallas kernels: 0 us -> 40.7 us
  starting transfers between devices: 19.1 us -> 42.4 us
  local copies, waits for them, and re-layouts: 24.9 us -> 6.1 us
  between operations: 14.8 us -> 1.81 us
    ppermute x4 -> x24, waiting for transfers between devices: 674 us -> 106 us  [the longest x12 57.5 us: ring_swap(): return lax.ppermute(x, RING_AXES, [(i, i ^ k) for i in range(RING)])]
    psum x1 -> x0, waiting for transfers between devices: 122 us -> none  [shards(): difference = lax.psum(stacked, 'day')]
    dot_general x8 -> x0, matrix products: 50 us -> none  [the longest x2 19.8 us: shards(): jnp.einsum('nij,djcnf->dicnf', weighted[offset - 1], partner_list[offset...]
    pallas_call x0 -> x17, Pallas kernels: none -> 40.7 us  [the longest x4 11.9 us: powers(): call(kernel, grid=(steps,), out_shape=jax.ShapeDtypeStruct(shape, jnp.flo...]
    ppermute x4 -> x24, starting transfers between devices: 19.1 us -> 42.4 us  [the longest x12 19.2 us: ring_swap(): return lax.ppermute(x, RING_AXES, [(i, i ^ k) for i in range(RING)])]
  transfers between devices with their start and end apart: 5 -> 24, of which waited for: 5 -> 11; matrix products, arithmetic and copies ran while one was open for 2% -> 1% of each run, Pallas kernels for 0% -> 18%
where the time goes in v1:
time: 201 us; the launch traced here: 197 us
  waiting for transfers between devices  106 us (53%)
  starting transfers between devices  42.4 us (21%)
  Pallas kernels  40.7 us (20%)
  local copies, waits for them, and re-layouts  6.1 us (3%)
    ppermute x12, waiting for transfers between devices, ring_swap(): return lax.ppermute(x, RING_AXES, [(i, i ^ k) for i in range(RING)])  57.5 us
    ppermute x5, waiting for transfers between devices, move_up(): lax.ppermute(x, 'h', [(i, (i + 1) % columns) for i in range(columns)])  40.5 us
    ppermute x12, starting transfers between devices, ring_swap(): return lax.ppermute(x, RING_AXES, [(i, i ^ k) for i in range(RING)])  19.2 us
    ppermute x5, starting transfers between devices, move_down(): lax.ppermute(x, 'h', [((i + 1) % columns, i) for i in range(columns)])  18.4 us
    pallas_call x4, Pallas kernels, powers(): call(kernel, grid=(steps,), out_shape=jax.ShapeDtypeStruct(shape, jnp.flo...  11.9 us
    pallas_call x4, Pallas kernels, gradients(): call(kernel, grid=(steps,), out_shape=[jax.ShapeDtypeStruct((rows, width)...  10 us
    pallas_call x3, Pallas kernels, pack(): call(kernel, out_shape=[jax.ShapeDtypeStruct((len(pieces) * rows + MASK_R...  9.06 us
    ppermute x5, waiting for transfers between devices, move_down(): lax.ppermute(x, 'h', [((i + 1) % columns, i) for i in range(columns)])  7.8 us
  transfers between devices with their start and end apart: 24, of which 11 were waited for; matrix products, arithmetic and copies ran while one was open for 1% of the time, Pallas kernels for 18%

profile of v1, /device:TPU:14, one launch (start us, length us, event | category | flops | bytes accessed | tf_op | source)
XLA Modules:
  0.0 197.5 jit_solution(7666274486610913368)
XLA Ops:
  0.0 3.1 %shard_map.47 = (bf16[256,1024]{1,0:T(8,128)(2,1)}, bf16[256,1024]{1,0:T(8,128)(2,1)}, bf16[256,1024]{1,0:T(8,128)(2,1)}) custom-call(bf16[2,1,128,8192]{3,2,1,0:T(8,128)(2,1)} %x_ref.5, s32[1,2]{1,0:T(1,128)} %m_ref.5), custom_call_target="tpu_custom_call" | custom-call | bytes 3145728 | tf_op jit(solution)/shard_map/pallas_call | solution.py:79
  4.6 3.1 %shard_map.51 = (bf16[256,1024]{1,0:T(8,128)(2,1)}, bf16[256,1024]{1,0:T(8,128)(2,1)}, bf16[264,1024]{1,0:T(8,128)(2,1)}) custom-call(bf16[2,1,128,8192]{3,2,1,0:T(8,128)(2,1)} %x_ref.5, s32[1,2]{1,0:T(1,128)} %m_ref.5), custom_call_target="tpu_custom_call" | custom-call | bytes 3145728 | tf_op jit(solution)/shard_map/pallas_call | solution.py:79
  7.8 2.7 %collective-permute-start.17 = (bf16[256,1024]{1,0:T(8,128)(2,1)}, bf16[256,1024]{1,0:T(8,128)(2,1)S(1)}, u32[]{:S(2)}, u32[]{:S(2)}) collective-permute-start(bf16[256,1024]{1,0:T(8,128)(2,1)} %get-tuple-element.28), channel_id=1, source_target_pairs={{0,6},{2,4},{4,2},{6,0},{1,7},{3,5},{5,3},{7,1},{8,14},{10,12},{12... | collective-permute-start | bytes 1572872 | tf_op jit(solution)/shard_map/ppermute | solution.py:311
  12.5 2.9 %shard_map.46.refs_0_.here_a = bf16[520,1024]{1,0:T(8,128)(2,1)} custom-call(bf16[2,1,128,8192]{3,2,1,0:T(8,128)(2,1)} %x_ref.5, s32[1,2]{1,0:T(1,128)} %m_ref.5), custom_call_target="tpu_custom_call" | custom-call | bytes 2097152 | tf_op jit(solution)/shard_map/pallas_call | solution.py:79
  15.3 4.4 %collective-permute-done.refs_1_ = bf16[256,1024]{1,0:T(8,128)(2,1)S(1)} collective-permute-done((bf16[256,1024]{1,0:T(8,128)(2,1)}, bf16[256,1024]{1,0:T(8,128)(2,1)S(1)}, u32[]{:S(2)}, u32[]{:S(2)}) %collective-permute-start) | collective-permute-done | bytes 524320 | tf_op jit(solution)/shard_map/ppermute | solution.py:311
  19.7 5.7 %collective-permute-start.1 = (bf16[520,1024]{1,0:T(8,128)(2,1)}, bf16[520,1024]{1,0:T(8,128)(2,1)S(1)}, u32[]{:S(2)}, u32[]{:S(2)}) collective-permute-start(bf16[520,1024]{1,0:T(8,128)(2,1)} %shard_map.46.refs_0_.here_a), channel_id=1, source_target_pairs={{8,0},{16,8},{24,16},{32,24},{40,32},{48,40},{56,48},{64,56},{72,6... | collective-permute-start | bytes 3194888 | tf_op jit(solution)/shard_map/ppermute | solution.py:319
  25.5 3.3 %collective-permute-done.16.refs_0_ = bf16[256,1024]{1,0:T(8,128)(2,1)S(1)} collective-permute-done((bf16[256,1024]{1,0:T(8,128)(2,1)}, bf16[256,1024]{1,0:T(8,128)(2,1)S(1)}, u32[]{:S(2)}, u32[]{:S(2)}) %collective-permute-start.16) | collective-permute-done | bytes 524320 | tf_op jit(solution)/shard_map/ppermute | solution.py:311
  32.3 3.6 %collective-permute-start.10 = (bf16[264,1024]{1,0:T(8,128)(2,1)}, bf16[264,1024]{1,0:T(8,128)(2,1)}, u32[]{:S(2)}, u32[]{:S(2)}) collective-permute-start(bf16[264,1024]{1,0:T(8,128)(2,1)} %get-tuple-element.22), channel_id=1, source_target_pairs={{0,4},{2,6},{4,0},{6,2},{1,5},{3,7},{5,1},{7,3},{8,12},{10,14},{12... | collective-permute-start | bytes 1622024 | tf_op jit(solution)/shard_map/ppermute | solution.py:311
  40.0 5.7 %collective-permute-start.18 = (bf16[512,1024]{1,0:T(8,128)(2,1)S(1)}, bf16[512,1024]{1,0:T(8,128)(2,1)}, u32[]{:S(2)}, u32[]{:S(2)}) collective-permute-start(bf16[512,1024]{1,0:T(8,128)(2,1)S(1)} %shard_map.55.refs_0_.refs_1_), channel_id=1, source_target_pairs={{8,0},{16,8},{24,16},{32,24},{40,32},{48,40},{56,48},{64,56},{72,6... | collective-permute-start | bytes 3145736 | tf_op jit(solution)/shard_map/ppermute | solution.py:319
  45.8 7.0 %collective-permute-done.10.here_b.refs_1_ = bf16[264,1024]{1,0:T(8,128)(2,1)} collective-permute-done((bf16[264,1024]{1,0:T(8,128)(2,1)}, bf16[264,1024]{1,0:T(8,128)(2,1)}, u32[]{:S(2)}, u32[]{:S(2)}) %collective-permute-start.10) | collective-permute-done | bytes 540704 | tf_op jit(solution)/shard_map/ppermute | solution.py:311
  57.8 3.8 %collective-permute-start.7 = (bf16[512,1024]{1,0:T(8,128)(2,1)}, bf16[512,1024]{1,0:T(8,128)(2,1)}, u32[]{:S(2)}, u32[]{:S(2)}) collective-permute-start(bf16[512,1024]{1,0:T(8,128)(2,1)} %shard_map.48.refs_0_.refs_1_), channel_id=1, source_target_pairs={{8,0},{16,8},{24,16},{32,24},{40,32},{48,40},{56,48},{64,56},{72,6... | collective-permute-start | bytes 3145736 | tf_op jit(solution)/shard_map/ppermute | solution.py:319
  63.7 30.3 %collective-permute-done.11.below_b.refs_5_ = bf16[264,1024]{1,0:T(8,128)(2,1)} collective-permute-done((bf16[264,1024]{1,0:T(8,128)(2,1)}, bf16[264,1024]{1,0:T(8,128)(2,1)}, u32[]{:S(2)}, u32[]{:S(2)}) %collective-permute-start.11) | collective-permute-done | bytes 540704 | tf_op jit(solution)/shard_map/ppermute | solution.py:315
  98.3 2.7 %shard_map.56.refs_6_ = f32[640,256]{1,0:T(8,128)S(1)} custom-call(f32[2,2]{1,0:T(2,128)S(1)} %get-tuple-element.36.w_ref, bf16[512,1024]{1,0:T(8,128)(2,1)S(1)} %shard_map.55.refs_0_.refs_1_, bf16[512,1024]{1,0:T(8,128)(2,1)S(1)} %shard_map.55.refs_0_.refs_1_, bf16[512,1024]{1,0:T(8,128)(2,1)} %collective-permute-done.18.refs_2_.refs_3_, ...), custom_call_target="tpu_custom_call" | custom-call | flops 805306368 | bytes 4194304 | tf_op jit(solution)/shard_map/pallas_call | solution.py:225
  100.9 7.8 %collective-permute-done.15.refs_3_ = bf16[264,1024]{1,0:T(8,128)(2,1)} collective-permute-done((bf16[264,1024]{1,0:T(8,128)(2,1)}, bf16[264,1024]{1,0:T(8,128)(2,1)}, u32[]{:S(2)}, u32[]{:S(2)}) %collective-permute-start.15) | collective-permute-done | bytes 540704 | tf_op jit(solution)/shard_map/ppermute | solution.py:319
  108.7 3.3 %shard_map.57.p_ref = f32[640,256]{1,0:T(8,128)} custom-call(f32[2,2]{1,0:T(2,128)S(1)} %get-tuple-element.36.w_ref, bf16[520,1024]{1,0:T(8,128)(2,1)S(1)} %copy-done, bf16[264,1024]{1,0:T(8,128)(2,1)} %collective-permute-done.10.here_b.refs_1_, bf16[520,1024]{1,0:T(8,128)(2,1)S(1)} %copy-done.2, bf16[264,1024]{1,0:T(8,128)(2,1)} %collective-permute-done.15.refs_3_, ...), custom_call_target="tpu_custom_call" | custom-call | flops 805306368 | bytes 4194304 | tf_op jit(solution)/shard_map/pallas_call | solution.py:225
  112.0 4.5 %collective-permute-done.8.refs_4_.refs_5_ = bf16[512,1024]{1,0:T(8,128)(2,1)} collective-permute-done((bf16[512,1024]{1,0:T(8,128)(2,1)}, bf16[512,1024]{1,0:T(8,128)(2,1)}, u32[]{:S(2)}, u32[]{:S(2)}) %collective-permute-start.8) | collective-permute-done | bytes 1048608 | tf_op jit(solution)/shard_map/ppermute | solution.py:315
  116.5 2.7 %shard_map.49.refs_6_ = f32[640,256]{1,0:T(8,128)S(1)} custom-call(f32[2,2]{1,0:T(2,128)S(1)} %get-tuple-element.36.w_ref, bf16[512,1024]{1,0:T(8,128)(2,1)} %shard_map.48.refs_0_.refs_1_, bf16[512,1024]{1,0:T(8,128)(2,1)} %shard_map.48.refs_0_.refs_1_, bf16[512,1024]{1,0:T(8,128)(2,1)} %collective-permute-done.7.refs_2_.refs_3_, ...), custom_call_target="tpu_custom_call" | custom-call | flops 805306368 | bytes 4194304 | tf_op jit(solution)/shard_map/pallas_call | solution.py:225
  119.3 5.7 %collective-permute-done.4.refs_5_ = bf16[256,1024]{1,0:T(8,128)(2,1)} collective-permute-done((bf16[256,1024]{1,0:T(8,128)(2,1)}, bf16[256,1024]{1,0:T(8,128)(2,1)}, u32[]{:S(2)}, u32[]{:S(2)}) %collective-permute-start.4) | collective-permute-done | bytes 524320 | tf_op jit(solution)/shard_map/ppermute | solution.py:315
  124.9 3.2 %shard_map.50.p_ref = f32[640,256]{1,0:T(8,128)} custom-call(f32[2,2]{1,0:T(2,128)S(1)} %get-tuple-element.36.w_ref, bf16[520,1024]{1,0:T(8,128)(2,1)S(1)} %copy-done, bf16[256,1024]{1,0:T(8,128)(2,1)S(1)} %copy-done.5, bf16[520,1024]{1,0:T(8,128)(2,1)S(1)} %copy-done.2, bf16[256,1024]{1,0:T(8,128)(2,1)} %collective-permute-done.2.refs_3_, ...), custom_call_target="tpu_custom_call" | custom-call | flops 805306368 | bytes 4194304 | tf_op jit(solution)/shard_map/pallas_call | solution.py:225
  138.4 2.7 %shard_map.54 = (bf16[256,1024]{1,0:T(8,128)(2,1)S(1)}, bf16[256,1024]{1,0:T(8,128)(2,1)S(1)}) custom-call(f32[2,2]{1,0:T(2,128)S(1)} %get-tuple-element.35.w_ref, bf16[3,256,256]{2,1,0:T(8,128)(2,1)S(1)} %shard_map.52.m_ref, bf16[512,1024]{1,0:T(8,128)(2,1)} %shard_map.48.refs_0_.refs_1_, bf16[512,1024]{1,0:T(8,128)(2,1)} %shard_map.48.refs_0_.refs_1_, ...), custom_call_target="tpu_custom_call" | custom-call | flops 805306368 | bytes 5242880 | tf_op jit(solution)/shard_map/pallas_call | solution.py:298
  143.7 3.6 %collective-permute-start.22 = (bf16[256,1024]{1,0:T(8,128)(2,1)S(1)}, bf16[256,1024]{1,0:T(8,128)(2,1)S(1)}, u32[]{:S(2)}, u32[]{:S(2)}) collective-permute-start(bf16[256,1024]{1,0:T(8,128)(2,1)S(1)} %get-tuple-element.31), channel_id=1, source_target_pairs={{0,4},{2,6},{4,0},{6,2},{1,5},{3,7},{5,1},{7,3},{8,12},{10,14},{12... | collective-permute-start | bytes 1572872 | tf_op jit(solution)/shard_map/ppermute | solution.py:311
  153.1 20.1 %collective-permute-done.22.refs_2_ = bf16[256,1024]{1,0:T(8,128)(2,1)S(1)} collective-permute-done((bf16[256,1024]{1,0:T(8,128)(2,1)S(1)}, bf16[256,1024]{1,0:T(8,128)(2,1)S(1)}, u32[]{:S(2)}, u32[]{:S(2)}) %collective-permute-start.22) | collective-permute-done | bytes 524320 | tf_op jit(solution)/shard_map/ppermute | solution.py:311
  173.2 12.6 %collective-permute-done.23.refs_3_ = bf16[256,1024]{1,0:T(8,128)(2,1)S(1)} collective-permute-done((bf16[256,1024]{1,0:T(8,128)(2,1)S(1)}, bf16[256,1024]{1,0:T(8,128)(2,1)S(1)}, u32[]{:S(2)}, u32[]{:S(2)}) %collective-permute-start.23) | collective-permute-done | bytes 524320 | tf_op jit(solution)/shard_map/ppermute | solution.py:311
  187.4 8.3 %collective-permute-done.14.refs_3_ = bf16[256,1024]{1,0:T(8,128)(2,1)S(1)} collective-permute-done((bf16[256,1024]{1,0:T(8,128)(2,1)S(1)}, bf16[256,1024]{1,0:T(8,128)(2,1)S(1)}, u32[]{:S(2)}, u32[]{:S(2)}) %collective-permute-start.14) | collective-permute-done | bytes 524320 | tf_op jit(solution)/shard_map/ppermute | solution.py:311
  (77 shorter events, 42.8 us)
Async XLA Ops:
  3.1 16.6 %collective-permute-start = (bf16[256,1024]{1,0:T(8,128)(2,1)}, bf16[256,1024]{1,0:T(8,128)(2,1)S(1)}, u32[]{:S(2)}, u32[]{:S(2)}) collective-permute-start(bf16[256,1024]{1,0:T(8,128)(2,1)} %get-tuple-element.19), channel_id=1, source_target_pairs={{0,4},{2,6},{4,0},{6,2},{1,5},{3,7},{5,1},{7,3},{8,12},{10,14},{12... | collective-permute-start | bytes 1572872 | tf_op jit(solution)/shard_map/ppermute | solution.py:311
  7.7 21.1 %collective-permute-start.16 = (bf16[256,1024]{1,0:T(8,128)(2,1)}, bf16[256,1024]{1,0:T(8,128)(2,1)S(1)}, u32[]{:S(2)}, u32[]{:S(2)}) collective-permute-start(bf16[256,1024]{1,0:T(8,128)(2,1)} %get-tuple-element.27), channel_id=1, source_target_pairs={{0,2},{2,0},{4,6},{6,4},{1,3},{3,1},{5,7},{7,5},{8,10},{10,8},{12,... | collective-permute-start | bytes 1572872 | tf_op jit(solution)/shard_map/ppermute | solution.py:311
  7.8 23.7 %collective-permute-start.17 = (bf16[256,1024]{1,0:T(8,128)(2,1)}, bf16[256,1024]{1,0:T(8,128)(2,1)S(1)}, u32[]{:S(2)}, u32[]{:S(2)}) collective-permute-start(bf16[256,1024]{1,0:T(8,128)(2,1)} %get-tuple-element.28), channel_id=1, source_target_pairs={{0,6},{2,4},{4,2},{6,0},{1,7},{3,5},{5,3},{7,1},{8,14},{10,12},{12... | collective-permute-start | bytes 1572872 | tf_op jit(solution)/shard_map/ppermute | solution.py:311
  10.5 29.5 %collective-permute-start.5 = (bf16[256,1024]{1,0:T(8,128)(2,1)}, bf16[256,1024]{1,0:T(8,128)(2,1)S(1)}, u32[]{:S(2)}, u32[]{:S(2)}) collective-permute-start(bf16[256,1024]{1,0:T(8,128)(2,1)} %get-tuple-element.20), channel_id=1, source_target_pairs={{0,2},{2,0},{4,6},{6,4},{1,3},{3,1},{5,7},{7,5},{8,10},{10,8},{12,... | collective-permute-start | bytes 1572872 | tf_op jit(solution)/shard_map/ppermute | solution.py:311
  11.3 34.4 %collective-permute-start.6 = (bf16[256,1024]{1,0:T(8,128)(2,1)}, bf16[256,1024]{1,0:T(8,128)(2,1)}, u32[]{:S(2)}, u32[]{:S(2)}) collective-permute-start(bf16[256,1024]{1,0:T(8,128)(2,1)} %get-tuple-element.21), channel_id=1, source_target_pairs={{0,6},{2,4},{4,2},{6,0},{1,7},{3,5},{5,3},{7,1},{8,14},{10,12},{12... | collective-permute-start | bytes 1572872 | tf_op jit(solution)/shard_map/ppermute | solution.py:311
  19.7 37.1 %collective-permute-start.1 = (bf16[520,1024]{1,0:T(8,128)(2,1)}, bf16[520,1024]{1,0:T(8,128)(2,1)S(1)}, u32[]{:S(2)}, u32[]{:S(2)}) collective-permute-start(bf16[520,1024]{1,0:T(8,128)(2,1)} %shard_map.46.refs_0_.here_a), channel_id=1, source_target_pairs={{8,0},{16,8},{24,16},{32,24},{40,32},{48,40},{56,48},{64,56},{72,6... | collective-permute-start | bytes 3194888 | tf_op jit(solution)/shard_map/ppermute | solution.py:319
  29.6 32.1 %collective-permute-start.3 = (bf16[520,1024]{1,0:T(8,128)(2,1)}, bf16[520,1024]{1,0:T(8,128)(2,1)S(1)}, u32[]{:S(2)}, u32[]{:S(2)}) collective-permute-start(bf16[520,1024]{1,0:T(8,128)(2,1)} %shard_map.46.refs_0_.here_a), channel_id=1, source_target_pairs={{0,8},{8,16},{16,24},{24,32},{32,40},{40,48},{48,56},{56,64},{64,7... | collective-permute-start | bytes 3194888 | tf_op jit(solution)/shard_map/ppermute | solution.py:315
  32.3 20.5 %collective-permute-start.10 = (bf16[264,1024]{1,0:T(8,128)(2,1)}, bf16[264,1024]{1,0:T(8,128)(2,1)}, u32[]{:S(2)}, u32[]{:S(2)}) collective-permute-start(bf16[264,1024]{1,0:T(8,128)(2,1)} %get-tuple-element.22), channel_id=1, source_target_pairs={{0,4},{2,6},{4,0},{6,2},{1,5},{3,7},{5,1},{7,3},{8,12},{10,14},{12... | collective-permute-start | bytes 1622024 | tf_op jit(solution)/shard_map/ppermute | solution.py:311
  40.0 56.2 %collective-permute-start.18 = (bf16[512,1024]{1,0:T(8,128)(2,1)S(1)}, bf16[512,1024]{1,0:T(8,128)(2,1)}, u32[]{:S(2)}, u32[]{:S(2)}) collective-permute-start(bf16[512,1024]{1,0:T(8,128)(2,1)S(1)} %shard_map.55.refs_0_.refs_1_), channel_id=1, source_target_pairs={{8,0},{16,8},{24,16},{32,24},{40,32},{48,40},{56,48},{64,56},{72,6... | collective-permute-start | bytes 3145736 | tf_op jit(solution)/shard_map/ppermute | solution.py:319
  45.8 51.4 %collective-permute-start.19 = (bf16[512,1024]{1,0:T(8,128)(2,1)S(1)}, bf16[512,1024]{1,0:T(8,128)(2,1)}, u32[]{:S(2)}, u32[]{:S(2)}) collective-permute-start(bf16[512,1024]{1,0:T(8,128)(2,1)S(1)} %shard_map.55.refs_0_.refs_1_), channel_id=1, source_target_pairs={{0,8},{8,16},{16,24},{24,32},{32,40},{40,48},{48,56},{56,64},{64,7... | collective-permute-start | bytes 3145736 | tf_op jit(solution)/shard_map/ppermute | solution.py:315
  52.8 41.3 %collective-permute-start.11 = (bf16[264,1024]{1,0:T(8,128)(2,1)}, bf16[264,1024]{1,0:T(8,128)(2,1)}, u32[]{:S(2)}, u32[]{:S(2)}) collective-permute-start(bf16[264,1024]{1,0:T(8,128)(2,1)} %collective-permute-done.10.here_b.refs_1_), channel_id=1, source_target_pairs={{0,8},{8,16},{16,24},{24,32},{32,40},{40,48},{48,56},{56,64},{64,7... | collective-permute-start | bytes 1622024 | tf_op jit(solution)/shard_map/ppermute | solution.py:315
  57.8 54.2 %collective-permute-start.7 = (bf16[512,1024]{1,0:T(8,128)(2,1)}, bf16[512,1024]{1,0:T(8,128)(2,1)}, u32[]{:S(2)}, u32[]{:S(2)}) collective-permute-start(bf16[512,1024]{1,0:T(8,128)(2,1)} %shard_map.48.refs_0_.refs_1_), channel_id=1, source_target_pairs={{8,0},{16,8},{24,16},{32,24},{40,32},{48,40},{56,48},{64,56},{72,6... | collective-permute-start | bytes 3145736 | tf_op jit(solution)/shard_map/ppermute | solution.py:319
  61.6 54.9 %collective-permute-start.8 = (bf16[512,1024]{1,0:T(8,128)(2,1)}, bf16[512,1024]{1,0:T(8,128)(2,1)}, u32[]{:S(2)}, u32[]{:S(2)}) collective-permute-start(bf16[512,1024]{1,0:T(8,128)(2,1)} %shard_map.48.refs_0_.refs_1_), channel_id=1, source_target_pairs={{0,8},{8,16},{16,24},{24,32},{32,40},{40,48},{48,56},{56,64},{64,7... | collective-permute-start | bytes 3145736 | tf_op jit(solution)/shard_map/ppermute | solution.py:315
  94.1 14.7 %collective-permute-start.15 = (bf16[264,1024]{1,0:T(8,128)(2,1)}, bf16[264,1024]{1,0:T(8,128)(2,1)}, u32[]{:S(2)}, u32[]{:S(2)}) collective-permute-start(bf16[264,1024]{1,0:T(8,128)(2,1)} %collective-permute-done.10.here_b.refs_1_), channel_id=1, source_target_pairs={{8,0},{16,8},{24,16},{32,24},{40,32},{48,40},{56,48},{64,56},{72,6... | collective-permute-start | bytes 1622024 | tf_op jit(solution)/shard_map/ppermute | solution.py:319
  96.2 23.1 %collective-permute-start.2 = (bf16[256,1024]{1,0:T(8,128)(2,1)}, bf16[256,1024]{1,0:T(8,128)(2,1)}, u32[]{:S(2)}, u32[]{:S(2)}) collective-permute-start(bf16[256,1024]{1,0:T(8,128)(2,1)} %copy-done.4), channel_id=1, source_target_pairs={{8,0},{16,8},{24,16},{32,24},{40,32},{48,40},{56,48},{64,56},{72,6... | collective-permute-start | bytes 1572872 | tf_op jit(solution)/shard_map/ppermute | solution.py:319
  97.2 27.7 %collective-permute-start.4 = (bf16[256,1024]{1,0:T(8,128)(2,1)}, bf16[256,1024]{1,0:T(8,128)(2,1)}, u32[]{:S(2)}, u32[]{:S(2)}) collective-permute-start(bf16[256,1024]{1,0:T(8,128)(2,1)} %copy-done.4), channel_id=1, source_target_pairs={{0,8},{8,16},{16,24},{24,32},{32,40},{40,48},{48,56},{56,64},{64,7... | collective-permute-start | bytes 1572872 | tf_op jit(solution)/shard_map/ppermute | solution.py:315
  112.0 16.9 %collective-permute-start.20 = (f32[640,256]{1,0:T(8,128)}, f32[640,256]{1,0:T(8,128)}, u32[]{:S(2)}, u32[]{:S(2)}) collective-permute-start(f32[640,256]{1,0:T(8,128)} %shard_map.57.p_ref), channel_id=1, source_target_pairs={{0,1},{1,0},{2,3},{3,2},{4,5},{5,4},{6,7},{7,6},{8,9},{9,8},{10,11... | collective-permute-start | bytes 1966088 | tf_op jit(solution)/shard_map/ppermute | solution.py:323
  128.2 8.1 %collective-permute-start.9 = (f32[640,256]{1,0:T(8,128)}, f32[640,256]{1,0:T(8,128)}, u32[]{:S(2)}, u32[]{:S(2)}) collective-permute-start(f32[640,256]{1,0:T(8,128)} %shard_map.50.p_ref), channel_id=1, source_target_pairs={{0,1},{1,0},{2,3},{3,2},{4,5},{5,4},{6,7},{7,6},{8,9},{9,8},{10,11... | collective-permute-start | bytes 1966088 | tf_op jit(solution)/shard_map/ppermute | solution.py:323
  133.5 18.3 %collective-permute-start.21 = (bf16[256,1024]{1,0:T(8,128)(2,1)S(1)}, bf16[256,1024]{1,0:T(8,128)(2,1)S(1)}, u32[]{:S(2)}, u32[]{:S(2)}) collective-permute-start(bf16[256,1024]{1,0:T(8,128)(2,1)S(1)} %get-tuple-element.30), channel_id=1, source_target_pairs={{0,2},{2,0},{4,6},{6,4},{1,3},{3,1},{5,7},{7,5},{8,10},{10,8},{12,... | collective-permute-start | bytes 1572872 | tf_op jit(solution)/shard_map/ppermute | solution.py:311
  141.2 46.2 %collective-permute-start.12 = (bf16[256,1024]{1,0:T(8,128)(2,1)S(1)}, bf16[256,1024]{1,0:T(8,128)(2,1)S(1)}, u32[]{:S(2)}, u32[]{:S(2)}) collective-permute-start(bf16[256,1024]{1,0:T(8,128)(2,1)S(1)} %get-tuple-element.24), channel_id=1, source_target_pairs={{0,2},{2,0},{4,6},{6,4},{1,3},{3,1},{5,7},{7,5},{8,10},{10,8},{12,... | collective-permute-start | bytes 1572872 | tf_op jit(solution)/shard_map/ppermute | solution.py:311
  143.7 29.5 %collective-permute-start.22 = (bf16[256,1024]{1,0:T(8,128)(2,1)S(1)}, bf16[256,1024]{1,0:T(8,128)(2,1)S(1)}, u32[]{:S(2)}, u32[]{:S(2)}) collective-permute-start(bf16[256,1024]{1,0:T(8,128)(2,1)S(1)} %get-tuple-element.31), channel_id=1, source_target_pairs={{0,4},{2,6},{4,0},{6,2},{1,5},{3,7},{5,1},{7,3},{8,12},{10,14},{12... | collective-permute-start | bytes 1572872 | tf_op jit(solution)/shard_map/ppermute | solution.py:311
  147.3 38.5 %collective-permute-start.23 = (bf16[256,1024]{1,0:T(8,128)(2,1)S(1)}, bf16[256,1024]{1,0:T(8,128)(2,1)S(1)}, u32[]{:S(2)}, u32[]{:S(2)}) collective-permute-start(bf16[256,1024]{1,0:T(8,128)(2,1)S(1)} %get-tuple-element.32), channel_id=1, source_target_pairs={{0,6},{2,4},{4,2},{6,0},{1,7},{3,5},{5,3},{7,1},{8,14},{10,12},{12... | collective-permute-start | bytes 1572872 | tf_op jit(solution)/shard_map/ppermute | solution.py:311
  150.8 36.6 %collective-permute-start.13 = (bf16[256,1024]{1,0:T(8,128)(2,1)S(1)}, bf16[256,1024]{1,0:T(8,128)(2,1)S(1)}, u32[]{:S(2)}, u32[]{:S(2)}) collective-permute-start(bf16[256,1024]{1,0:T(8,128)(2,1)S(1)} %get-tuple-element.25), channel_id=1, source_target_pairs={{0,4},{2,6},{4,0},{6,2},{1,5},{3,7},{5,1},{7,3},{8,12},{10,14},{12... | collective-permute-start | bytes 1572872 | tf_op jit(solution)/shard_map/ppermute | solution.py:311
  151.8 43.9 %collective-permute-start.14 = (bf16[256,1024]{1,0:T(8,128)(2,1)S(1)}, bf16[256,1024]{1,0:T(8,128)(2,1)S(1)}, u32[]{:S(2)}, u32[]{:S(2)}) collective-permute-start(bf16[256,1024]{1,0:T(8,128)(2,1)S(1)} %get-tuple-element.26), channel_id=1, source_target_pairs={{0,6},{2,4},{4,2},{6,0},{1,7},{3,5},{5,3},{7,1},{8,14},{10,12},{12... | collective-permute-start | bytes 1572872 | tf_op jit(solution)/shard_map/ppermute | solution.py:311
  (13 other events, 173.7 us)
